TPU v7x, 32 devices: a whole 2x2x4 slice. The times are simulated.
32 devices in a mesh: parts: 2 (over y), blk: 4 (over z), row: 2 (over x), sub: 2 (over core).
Axes of the slice: x: 2, y: 2, z: 4, core: 2. Of those that a mesh axis runs over, the one named last changes fastest.
Arguments:
- query_grads: bfloat16 [512, 4, 2048], P('blk', None, 'sub'), may hold values from -6 to 6
- curvature: bfloat16 [4, 2048, 2048], P('blk', ('row', 'sub')), may hold values from -0.125 to 0.125
- train_grads: bfloat16 [5120, 4, 2048], P(('parts', 'row', 'sub'), 'blk'), parts along dimension 0, may hold values from -0.0625 to 0.0625
- query_ids: int32 [1024], P('parts'), parts along dimension 0, may hold values from 0 to 511, each once
- block_map: int32 [4], replicated, may hold values from 0 to 3, each once
- row_ids: int32 [5120], P(('parts', 'row', 'sub')), parts along dimension 0, may hold values from 0 to 639
Outputs:
- scores: float32 [512, 5120], P('blk', ('parts', 'row', 'sub')), parts along dimension 1
There are 2 independent parts, one for each index of `parts`. A program takes and returns all parts, laid end to end along the dimension named above; an argument that names none is the same for every part. Nothing has to cross between parts.
Inputs may be any that keep to these rules, and one draw needn't show every extreme that they name: `query_ids`: each value appears once. `block_map`: each value appears once.
All inputs are finite; a program needn't handle non-finite values.
Results may differ from a plain program's by a relative error of at most 0.0029.
Values may be sent and summed in bfloat16 or wider, within the bound.
No kernel may reach another device: no remote copies, remote signals or barrier semaphores. Data moves between devices by JAX's collectives and lax.ppermute only.
A program may use at most 64 MiB of HBM per device.

v0:
```python
import jax
import jax.numpy as jnp
from jax import lax
from jax.sharding import PartitionSpec as P


def per_device(query_grads, curvature, train_grads, query_ids, block_map, row_ids):
    mine = jnp.take(query_grads, block_map, axis=1)
    arrived = lax.all_to_all(mine, "blk", split_axis=1, concat_axis=0, tiled=True)
    queries = arrived.shape[0]
    precond = jnp.einsum(
        "qsj,sij->qsi",
        lax.all_gather(arrived, "sub", axis=2, tiled=True),
        curvature,
        preferred_element_type=jnp.float32,
    ).astype(jnp.bfloat16)
    inverse = (
        jnp.zeros((queries,), jnp.int32).at[query_ids].set(jnp.arange(queries, dtype=jnp.int32))
    )
    ordered = jnp.take(precond, inverse, axis=0)
    chosen = jnp.take(train_grads, row_ids, axis=0)
    partial_value = jnp.einsum(
        "qsk,rsk->qr",
        lax.all_gather(ordered, ("row", "sub"), axis=2, tiled=True),
        chosen,
        preferred_element_type=jnp.float32,
    )
    return lax.psum_scatter(partial_value, "blk", scatter_dimension=0, tiled=True)


def solution(mesh):
    placed = (
        P("blk", None, "sub"),
        P("blk", ("row", "sub"), None),
        P(("parts", "row", "sub"), "blk", None),
        P("parts"),
        P(),
        P(("parts", "row", "sub")),
    )
    return jax.shard_map(
        per_device,
        mesh=mesh,
        in_specs=placed,
        out_specs=P("blk", ("parts", "row", "sub")),
        check_vma=False,
    )
```

profile of v0, /device:TPU:0, one launch (start us, length us, event | category | flops | bytes accessed | tf_op | source)
XLA Modules:
  0.0 133.5 jit_solution(11992758323479835850)
XLA Ops:
  6.5 0.0 copy-start
  6.5 0.0 all-gather.3.cloned.1.call-start
  6.5 0.8 compare_and_fusion.1
  7.4 0.7 compare_select_fusion.3
  8.0 6.1 %gather_fusion = bf16[4,128,1024]{2,0,1:T(4,128)(2,1)} fusion(bf16[128,4,1024]{2,1,0:T(4,128)(2,1)} %param.6, s32[1024]{0:T(1024)S(1)} %pad_clamp_fusion.2), kind=kCustom, calls=%fused_computation | custom fusion | bytes 2097168 | tf_op jit(solution)/shard_map/jit(_take)/gather | solution.py:8
  14.1 1.7 %select_bitcast_fusion = bf16[128,4,1024]{2,1,0:T(4,128)(2,1)S(1)} fusion(bf16[4,128,1024]{2,0,1:T(4,128)(2,1)} %gather_fusion, pred[4]{0:T(512)(128)(4,1)S(1)} %compare_and_fusion.1), kind=kLoop, calls=%fused_computation.14 | loop fusion | flops 524288 | bytes 2097156 | tf_op jit(solution)/shard_map/jit(_take)/select_n | solution.py:8
  15.9 0.3 copy.8
  16.2 0.0 copy-start.2
  16.2 32.0 %all_to_all.18 = bf16[128,4,1024]{2,0,1:T(8,128)(2,1)} all-to-all(bf16[128,4,1024]{2,0,1:T(8,128)(2,1)S(1)} %copy.8), channel_id=1, replica_groups=mesh['parts'=2,'blk'=4,'row'=2,'sub'=2] {'blk'}, dimensions={1} | all-to-all | bytes 2097152 | tf_op jit(solution)/shard_map/all_to_all | solution.py:9
  48.2 0.0 all-gather.3.cloned.1.call-update
  48.2 0.0 all-gather.5.cloned.1.call-start
  48.2 0.0 copy-done.2
  48.3 2.4 %scatter_custom_fusion = s32[512]{0:T(512)S(1)} fusion(s32[512]{0:T(512)S(1)} %compare_select_fusion.2, s32[512]{0:T(512)S(1)} %iota.3, s32[]{:T(128)} %constant.30.clone.1), kind=kCustom, calls=%fused_computation.26 | custom fusion | bytes 2052 | tf_op jit(solution)/shard_map/scatter | solution.py:18
  50.8 7.3 %all-gather.3.cloned.1.call-done = bf16[512,1,2048]{2,0,1:T(8,128)(2,1)} async-done(((bf16[512,1,1024]{2,0,1:T(8,128)(2,1)}), bf16[512,1,2048]{2,0,1:T(8,128)(2,1)}) %all-gather.3.cloned.1.call-update) | async-done | bytes 2097168 | tf_op jit(solution)/shard_map/all_gather | solution.py:13
  58.0 3.5 %fusion.8 = bf16[512,512]{1,0:T(8,128)(2,1)S(1)} fusion(bf16[1,512,2048]{2,1,0:T(8,128)(2,1)} %param.7, bf16[512,1,2048]{2,0,1:T(8,128)(2,1)} %all-gather.3.cloned.1.call-done), kind=kOutput, calls=%fused_computation.13 | convolution fusion | flops 1074003968 | bytes 4718592 | tf_op jit(solution)/shard_map/qsj,sij->qsi/dot_general | solution.py:11
  61.5 0.0 copy-start.1
  61.6 2.6 %gather_fusion.1 = bf16[512,512]{1,0:T(8,128)(2,1)} fusion(bf16[512,512]{1,0:T(8,128)(2,1)S(1)} %fusion.8, s32[1024]{0:T(1024)S(1)} %pad_clamp_fusion.1), kind=kCustom, calls=%fused_computation.1 | custom fusion | bytes 1050624 | tf_op jit(solution)/shard_map/jit(_take)/gather | solution.py:20
  64.2 2.0 %bitcast_select_fusion.2 = bf16[512,1,512]{2,0,1:T(8,128)(2,1)} fusion(bf16[512,512]{1,0:T(8,128)(2,1)} %gather_fusion.1, pred[512]{0:T(512)(128)(4,1)S(1)} %compare_and_fusion.2), kind=kLoop, calls=%fused_computation.15 | loop fusion | flops 262144 | bytes 1049088 | tf_op jit(solution)/shard_map/jit(_take)/select_n | solution.py:20
  66.2 0.0 all-gather.5.cloned.1.call-update
  66.2 0.0 reduce-scatter.2.cloned.1.call-start
  66.2 0.0 copy-done.1
  66.3 0.0 copy-done
  66.3 4.1 %gather_fusion.2 = bf16[640,2048]{1,0:T(8,128)(2,1)} fusion(bf16[640,2048]{1,0:T(8,128)(2,1)S(1)} %bitcast.32, s32[1024]{0:T(1024)S(1)} %pad_clamp_fusion), kind=kCustom, calls=%fused_computation.2 | custom fusion | bytes 5245440 | tf_op jit(solution)/shard_map/jit(_take)/gather | solution.py:21
  70.3 19.7 %all-gather.5.cloned.1.call-done = bf16[512,1,2048]{2,0,1:T(8,128)(2,1)} async-done(((bf16[512,1,512]{2,0,1:T(8,128)(2,1)}), bf16[512,1,2048]{2,0,1:T(8,128)(2,1)}) %all-gather.5.cloned.1.call-update) | async-done | bytes 2097168 | tf_op jit(solution)/shard_map/all_gather | solution.py:24
  90.1 5.4 %fusion = f32[512,640]{1,0:T(8,128)} fusion(bf16[640,2048]{1,0:T(8,128)(2,1)} %gather_fusion.2, pred[640]{0:T(1024)(128)(4,1)S(1)} %compare_and_fusion, bf16[512,1,2048]{2,0,1:T(8,128)(2,1)} %all-gather.5.cloned.1.call-done), kind=kOutput, calls=%fused_computation.4 | convolution fusion | flops 1343488000 | bytes 6029952 | tf_op jit(solution)/shard_map/qsk,rsk->qr/dot_general | solution.py:22
  95.5 0.0 reduce-scatter.2.cloned.1.call-update
  95.5 31.5 %reduce-scatter.2.cloned.1.call-done = f32[128,640]{1,0:T(8,128)} async-done(((f32[512,640]{1,0:T(8,128)}), f32[128,640]{1,0:T(8,128)}) %reduce-scatter.2.cloned.1.call-update) | async-done | bytes 327696 | tf_op jit(solution)/shard_map/reduce_scatter | solution.py:28
  (9 shorter events, 0.0 us)
Async XLA Ops:
  6.5 59.7 %copy-start = (bf16[640,1,2048]{2,0,1:T(8,128)(2,1)S(1)}, bf16[640,1,2048]{2,0,1:T(8,128)(2,1)}, u32[]{:S(2)}) copy-start(bf16[640,1,2048]{2,0,1:T(8,128)(2,1)} %param.8) | copy-start | bytes 7864324
  6.5 51.5 %all-gather.3.cloned.1.call-start = ((), (), s32[]{:S(2)}) async-start(), calls=%async_computation.2 | async-start | bytes 3145728 | tf_op jit(solution)/shard_map/all_gather | solution.py:13
  16.2 32.1 %copy-start.2 = (s32[512]{0:T(512)S(1)}, s32[512]{0:T(512)}, u32[]{:S(2)}) copy-start(s32[512]{0:T(512)} %param.9) | copy-start | bytes 6148
  48.2 41.9 %all-gather.5.cloned.1.call-start = ((), (), s32[]{:S(2)}) async-start(), calls=%async_computation.3 | async-start | bytes 2621440 | tf_op jit(solution)/shard_map/all_gather | solution.py:24
  61.5 4.7 %copy-start.1 = (s32[640]{0:T(1024)S(1)}, s32[640]{0:T(1024)}, u32[]{:S(2)}) copy-start(s32[640]{0:T(1024)} %param.11) | copy-start | bytes 7684
  66.2 60.8 %reduce-scatter.2.cloned.1.call-start = ((), (), s32[]{:S(2)}) async-start(), calls=%async_computation.4 | async-start | bytes 1638400 | tf_op jit(solution)/shard_map/reduce_scatter | solution.py:28
Sparse Core Ops, SparseCore 0:
  48.3 9.6 all-gather.2
  66.3 23.7 all-gather.4
  95.6 31.3 reduce-scatter.1
where the time goes:
time: 134 us
  waiting for transfers between devices  58.6 us (44%)
  blocking collectives  32 us (24%)
  local copies, waits for them, and re-layouts  15.6 us (12%)
  between operations  13.2 us (10%)
  matrix products  8.89 us (7%)
  other arithmetic  5.23 us (4%)
    all_to_all x1, blocking collectives, per_device(): lax.all_to_all(mine, 'blk', split_axis=1, concat_axis=0, tiled=True)  32 us
    reduce_scatter x1, waiting for transfers between devices, per_device(): lax.psum_scatter(partial_value, 'blk', scatter_dimension=0, tiled=True)  31.5 us
    all_gather x1, waiting for transfers between devices, per_device(): lax.all_gather(ordered, ('row', 'sub'), axis=2, tiled=True)  19.7 us
    all_gather x1, waiting for transfers between devices, per_device(): lax.all_gather(arrived, 'sub', axis=2, tiled=True)  7.27 us
    gather x1, local copies, waits for them, and re-layouts, per_device(): mine = jnp.take(query_grads, block_map, axis=1)  6.1 us
    dot_general x1, matrix products, per_device(): jnp.einsum('qsk,rsk->qr', lax.all_gather(ordered, ('row', 'sub'), axis=2,...  5.39 us
    gather x1, local copies, waits for them, and re-layouts, per_device(): chosen = jnp.take(train_grads, row_ids, axis=0)  4.06 us
    dot_general x1, matrix products, per_device(): jnp.einsum('qsj,sij->qsi', lax.all_gather(arrived, 'sub', axis=2, tiled=T...  3.5 us
  transfers between devices with their start and end apart: 3, of which 3 were waited for; matrix products, arithmetic and copies ran while one was open for 5% of the time, Pallas kernels for 0%

commit v1 on v0

v1 whole, which is shorter than its diff:
```python
import functools

import jax
import jax.numpy as jnp
from jax import lax
from jax.sharding import PartitionSpec as P


def swaps(n):
    if n & (n - 1) == 0:
        return [(lambda i, d=d: i ^ d) for d in range(n)], [(lambda i, d=d: i ^ d) for d in range(n)]
    return [(lambda i, d=d: (i + d) % n) for d in range(n)], [(lambda i, d=d: (i - d) % n) for d in range(n)]


def per_device(sizes, query_grads, curvature, train_grads, query_ids, block_map, row_ids):
    n_parts, n_blk, n_row, n_sub = (sizes[a] for a in ("parts", "blk", "row", "sub"))
    part, blk, row, sub = (lax.axis_index(a) for a in ("parts", "blk", "row", "sub"))
    to_part, from_part = swaps(n_parts)
    to_blk, from_blk = swaps(n_blk)
    to_row, from_row = swaps(n_row)
    to_sub, from_sub = swaps(n_sub)
    owned, half = query_grads.shape[0], query_grads.shape[2]
    mine_q = owned // n_parts
    n_feat = curvature.shape[1]
    queries = owned * n_blk

    def send(x, axes, pairs):
        return lax.ppermute(x, axes, pairs)

    blk_pairs = [[(i, to_blk[d](i)) for i in range(n_blk)] for d in range(n_blk)]
    sub_pairs = [[(i, to_sub[d](i)) for i in range(n_sub)] for d in range(n_sub)]

    def plane_pairs(dp, dr):
        return [
            (a * n_row + b, to_part[dp](a) * n_row + to_row[dr](b)) for a in range(n_parts) for b in range(n_row)
        ]

    by_block = jnp.swapaxes(lax.dynamic_slice_in_dim(query_grads, part * mine_q, mine_q, 0), 0, 1)
    arrived = []
    for d in range(n_blk):
        piece = lax.dynamic_index_in_dim(by_block, block_map[to_blk[d](blk)], 0, keepdims=False)
        arrived.append(send(piece, "blk", blk_pairs[d]) if d else piece)
    arrived = jnp.concatenate(arrived, 0)

    block = curvature[0]
    total = 0
    for d in range(n_sub):
        have = send(arrived, "sub", sub_pairs[d]) if d else arrived
        columns = lax.dynamic_slice_in_dim(block, from_sub[d](sub) * half, half, 1)
        total = total + jnp.einsum("qj,ij->qi", have, columns, preferred_element_type=jnp.float32)
    precond = total.astype(jnp.bfloat16)

    chosen = jnp.take(train_grads[:, 0], row_ids, axis=0, mode="clip")
    partial_rows, ids = [], []
    got = {}
    for dp in range(n_parts):
        for dr in range(n_row):
            got[dp, dr] = send(precond, ("parts", "row"), plane_pairs(dp, dr)) if dp or dr else precond
    flat = jnp.concatenate([got[dp, dr] for dp in range(n_parts) for dr in range(n_row)], 1)
    flats = [send(flat, "sub", sub_pairs[ds]) if ds else flat for ds in range(n_sub)]
    for dp in range(n_parts):
        scores = 0
        for ds in range(n_sub):
            for dr in range(n_row):
                there = (from_row[dr](row) * n_sub + from_sub[ds](sub)) * n_feat
                at = (dp * n_row + dr) * n_feat
                scores = scores + jnp.einsum(
                    "qk,rk->qr",
                    flats[ds][:, at : at + n_feat],
                    lax.dynamic_slice_in_dim(chosen, there, n_feat, 1),
                    preferred_element_type=jnp.float32,
                )
        partial_rows.append(scores.astype(jnp.bfloat16))
        for d in range(n_blk):
            start = from_blk[d](blk) * owned + from_part[dp](part) * mine_q
            ids.append(lax.dynamic_slice_in_dim(query_ids, start, mine_q, 0))
    partial_rows = jnp.concatenate(partial_rows, 0)
    ids = jnp.concatenate(ids, 0)

    out = 0
    for d in range(n_blk):
        rows = to_blk[d](blk) * owned + lax.broadcasted_iota(jnp.int32, (owned, queries), 0)
        pick = (rows == ids[None, :]).astype(jnp.bfloat16)
        placed = jnp.einsum("oq,qr->or", pick, partial_rows, preferred_element_type=jnp.float32)
        if d:
            placed = send(placed.astype(jnp.bfloat16), "blk", blk_pairs[d]).astype(jnp.float32)
        out = out + placed
    return out


def solution(mesh):
    placed = (
        P("blk", None, "sub"),
        P("blk", ("row", "sub"), None),
        P(("parts", "row", "sub"), "blk", None),
        P("parts"),
        P(),
        P(("parts", "row", "sub")),
    )
    return jax.shard_map(
        functools.partial(per_device, dict(mesh.shape)),
        mesh=mesh,
        in_specs=placed,
        out_specs=P("blk", ("parts", "row", "sub")),
        check_vma=False,
    )
```

time: 134 us -> 77.2 us (0.58)
  blocking collectives: 32 us -> 0 us
  waiting for transfers between devices: 58.6 us -> 32.1 us
  starting transfers between devices: 0.09 us -> 14.3 us
  local copies, waits for them, and re-layouts: 15.6 us -> 9.08 us
  between operations: 13.2 us -> 7.98 us
  other arithmetic: 5.23 us -> 2.83 us
  matrix products: 8.89 us -> 10.4 us
    ppermute x0 -> x11, waiting for transfers between devices: none -> 32.1 us  [send(): return lax.ppermute(x, axes, pairs)]
    all_to_all x1 -> x0, blocking collectives: 32 us -> none  [per_device(): lax.all_to_all(mine, 'blk', split_axis=1, concat_axis=0, tiled=True)]
    reduce_scatter x1 -> x0, waiting for transfers between devices: 31.5 us -> none  [per_device(): lax.psum_scatter(partial_value, 'blk', scatter_dimension=0, tiled=True)]
    all_gather x2 -> x0, waiting for transfers between devices: 27 us -> none  [the longest x1 19.7 us: per_device(): lax.all_gather(ordered, ('row', 'sub'), axis=2, tiled=True)]
    ppermute x0 -> x11, starting transfers between devices: none -> 14.3 us  [send(): return lax.ppermute(x, axes, pairs)]
    gather x3 -> x1, local copies, waits for them, and re-layouts: 12.8 us -> 4.08 us  [per_device(): chosen = jnp.take(train_grads[:, 0], row_ids, axis=0, mode='clip')]
    select_n x6 -> x0, other arithmetic: 4.39 us -> none  [the longest x2 2.4 us: per_device(): mine = jnp.take(query_grads, block_map, axis=1)]
    another operation x0 -> x1, local copies, waits for them, and re-layouts: none -> 3.1 us
  transfers between devices with their start and end apart: 3 -> 11, of which waited for: 3 -> 8; matrix products, arithmetic and copies ran while one was open for 5% -> 10% of each run, Pallas kernels for 0% -> 0%
where the time goes in v1:
time: 77.2 us; the launch traced here: 76.7 us
  waiting for transfers between devices  32.1 us (42%)
  starting transfers between devices  14.3 us (19%)
  matrix products  10.4 us (13%)
  local copies, waits for them, and re-layouts  9.08 us (12%)
  between operations  7.98 us (10%)
  other arithmetic  2.83 us (4%)
    ppermute x11, waiting for transfers between devices, send(): return lax.ppermute(x, axes, pairs)  32.1 us
    ppermute x11, starting transfers between devices, send(): return lax.ppermute(x, axes, pairs)  14.3 us
    dot_general x8, matrix products, per_device(): jnp.einsum('qk,rk->qr', flats[ds][:, at:at + n_feat], lax.dynamic_slice_i...  5.38 us
    gather x1, local copies, waits for them, and re-layouts, per_device(): chosen = jnp.take(train_grads[:, 0], row_ids, axis=0, mode='clip')  4.08 us
    another operation x1, local copies, waits for them, and re-layouts  3.1 us
    dot_general x2, matrix products, per_device(): jnp.einsum('qj,ij->qi', have, columns, preferred_element_type=jnp.float32)  3.08 us
    dot_general x4, matrix products, per_device(): jnp.einsum('oq,qr->or', pick, partial_rows, preferred_element_type=jnp.fl...  1.98 us
    concatenate x1, other arithmetic, per_device(): arrived = jnp.concatenate(arrived, 0)  1.75 us
  transfers between devices with their start and end apart: 11, of which 8 were waited for; matrix products, arithmetic and copies ran while one was open for 10% of the time, Pallas kernels for 0%

profile of v1, /device:TPU:0, one launch (start us, length us, event | category | flops | bytes accessed | tf_op | source)
XLA Modules:
  0.0 76.7 jit_solution(15709513255451646781)
XLA Ops:
  0.0 1.5 %fusion.54 = (s32[1]{0:T(128)}, s32[1]{0:T(128)}, s32[1]{0:T(128)}, s32[1]{0:T(128)}) fusion(s32[4]{0:T(128)} %param.10, s32[]{:T(128)S(6)} %select_n.94, s32[]{:T(128)S(6)} %select_n.97, s32[]{:T(128)S(6)} %select_n.103, s32[]{:T(128)S(6)} %select_n.100), kind=kLoop, calls=%fused_computation.77 | loop fusion | bytes 48 | tf_op jit(solution)/shard_map/dynamic_slice | solution.py:41
  9.3 3.1 %constant_dynamic-slice_fusion.3 = (bf16[64,1,1024]{2,1,0:T(2,128)(2,1)S(1)}, bf16[64,1,1024]{2,1,0:T(2,128)(2,1)S(1)}, bf16[64,1,1024]{2,1,0:T(2,128)(2,1)S(1)}, bf16[64,1,1024]{2,1,0:T(2,128)(2,1)S(1)}) fusion(bf16[128,4,1024]{2,1,0:T(4,128)(2,1)} %param.6, s32[]{:T(128)S(6)} %select_n.93, s32[]{:T(128)S(6)} %select_n.96, s32[]{:T(128)S(6)} %select_n.102, ...), kind=kLoop, calls=%fused_computation.71 | loop fusion | bytes 1048596 | tf_op jit(solution)/shard_map/dynamic-slice
  12.5 3.1 %collective-permute-start = (bf16[64,1024]{1,0:T(8,128)(2,1)S(1)}, bf16[64,1024]{1,0:T(8,128)(2,1)S(1)}, u32[]{:S(2)}, u32[]{:S(2)}) collective-permute-start(bf16[64,1024]{1,0:T(8,128)(2,1)S(1)} %bitcast.31), channel_id=1, source_target_pairs={{0,4},{4,0},{8,12},{12,8},{1,5},{5,1},{9,13},{13,9},{2,6},{6,2},{1... | collective-permute-start | bytes 393224 | tf_op jit(solution)/shard_map/ppermute | solution.py:28
  15.6 2.7 %collective-permute-start.1 = (bf16[64,1024]{1,0:T(8,128)(2,1)S(1)}, bf16[64,1024]{1,0:T(8,128)(2,1)S(1)}, u32[]{:S(2)}, u32[]{:S(2)}) collective-permute-start(bf16[64,1024]{1,0:T(8,128)(2,1)S(1)} %bitcast.32), channel_id=1, source_target_pairs={{0,8},{4,12},{8,0},{12,4},{1,9},{5,13},{9,1},{13,5},{2,10},{6,14},... | collective-permute-start | bytes 393224 | tf_op jit(solution)/shard_map/ppermute | solution.py:28
  18.3 0.1 collective-permute-start.2
  18.4 2.1 %collective-permute-done = bf16[64,1024]{1,0:T(8,128)(2,1)S(1)} collective-permute-done((bf16[64,1024]{1,0:T(8,128)(2,1)S(1)}, bf16[64,1024]{1,0:T(8,128)(2,1)S(1)}, u32[]{:S(2)}, u32[]{:S(2)}) %collective-permute-start) | collective-permute-done | bytes 131104 | tf_op jit(solution)/shard_map/ppermute | solution.py:28
  20.6 8.0 %collective-permute-done.1 = bf16[64,1024]{1,0:T(8,128)(2,1)S(1)} collective-permute-done((bf16[64,1024]{1,0:T(8,128)(2,1)S(1)}, bf16[64,1024]{1,0:T(8,128)(2,1)S(1)}, u32[]{:S(2)}, u32[]{:S(2)}) %collective-permute-start.1) | collective-permute-done | bytes 131104 | tf_op jit(solution)/shard_map/ppermute | solution.py:28
  28.6 0.0 collective-permute-done.2
  28.6 1.7 %pad_maximum_fusion.2 = bf16[256,1024]{1,0:T(8,128)(2,1)} fusion(bf16[64,1024]{1,0:T(8,128)(2,1)} %collective-permute-done.2, bf16[64,1024]{1,0:T(8,128)(2,1)S(1)} %collective-permute-done.1, bf16[64,1024]{1,0:T(8,128)(2,1)S(1)} %collective-permute-done, bf16[64,1024]{1,0:T(8,128)(2,1)S(1)} %bitcast.29), kind=kLoop, calls=%fused_computation.34 | loop fusion | flops 2097152 | bytes 1048576 | tf_op jit(solution)/shard_map/concatenate | solution.py:43
  30.3 0.0 collective-permute-start.3
  30.3 2.1 %collective-permute-done.3 = bf16[256,1024]{1,0:T(8,128)(2,1)S(1)} collective-permute-done((bf16[256,1024]{1,0:T(8,128)(2,1)}, bf16[256,1024]{1,0:T(8,128)(2,1)S(1)}, u32[]{:S(2)}, u32[]{:S(2)}) %collective-permute-start.3) | collective-permute-done | bytes 524320 | tf_op jit(solution)/shard_map/ppermute | solution.py:28
  32.4 1.7 %fusion.6 = f32[256,512]{1,0:T(8,128)S(1)} fusion(bf16[256,1024]{1,0:T(8,128)(2,1)S(1)} %collective-permute-done.3, bf16[1,512,2048]{2,1,0:T(8,128)(2,1)} %param.7, s32[]{:T(128)S(6)} %select_n.107), kind=kOutput, calls=%fused_computation.15 | convolution fusion | flops 268435456 | bytes 2097156 | tf_op jit(solution)/shard_map/qj,ij->qi/dot_general | solution.py:50
  34.1 0.0 copy-start.4
  34.2 1.4 %fusion.5 = bf16[256,512]{1,0:T(8,128)(2,1)S(1)} fusion(f32[256,512]{1,0:T(8,128)S(1)} %fusion.6, bf16[1,512,2048]{2,1,0:T(8,128)(2,1)S(1)} %copy-done.2, s32[]{:T(128)S(6)} %select_n.106, bf16[64,1024]{1,0:T(8,128)(2,1)} %collective-permute-done.2, bf16[64,1024]{1,0:T(8,128)(2,1)S(1)} %collective-permute-done.1, ...), kind=kOutput, calls=%fused_computation.10 | convolution fusion | flops 270794752 | bytes 2359300 | tf_op jit(solution)/shard_map/qj,ij->qi/dot_general | solution.py:50
  35.5 1.6 %collective-permute-start.4 = (bf16[256,512]{1,0:T(8,128)(2,1)S(1)}, bf16[256,512]{1,0:T(8,128)(2,1)S(1)}, u32[]{:S(2)}, u32[]{:S(2)}) collective-permute-start(bf16[256,512]{1,0:T(8,128)(2,1)S(1)} %fusion.5), channel_id=1, source_target_pairs={{0,2},{2,0},{16,18},{18,16},{1,3},{3,1},{17,19},{19,17},{4,6},{6,4... | collective-permute-start | bytes 786440 | tf_op jit(solution)/shard_map/ppermute | solution.py:28
  37.1 1.2 %collective-permute-start.5 = (bf16[256,512]{1,0:T(8,128)(2,1)S(1)}, bf16[256,512]{1,0:T(8,128)(2,1)}, u32[]{:S(2)}, u32[]{:S(2)}) collective-permute-start(bf16[256,512]{1,0:T(8,128)(2,1)S(1)} %fusion.5), channel_id=1, source_target_pairs={{0,16},{2,18},{16,0},{18,2},{1,17},{3,19},{17,1},{19,3},{4,20},{6,... | collective-permute-start | bytes 786440 | tf_op jit(solution)/shard_map/ppermute | solution.py:28
  38.3 0.8 %collective-permute-start.6 = (bf16[256,512]{1,0:T(8,128)(2,1)S(1)}, bf16[256,512]{1,0:T(8,128)(2,1)S(1)}, u32[]{:S(2)}, u32[]{:S(2)}) collective-permute-start(bf16[256,512]{1,0:T(8,128)(2,1)S(1)} %fusion.5), channel_id=1, source_target_pairs={{0,18},{2,16},{16,2},{18,0},{1,19},{3,17},{17,3},{19,1},{4,22},{6,... | collective-permute-start | bytes 786440 | tf_op jit(solution)/shard_map/ppermute | solution.py:28
  39.1 0.0 copy-done
  39.1 0.0 copy-start.3
  39.1 4.1 %gather_fusion = bf16[640,2048]{1,0:T(8,128)(2,1)} fusion(bf16[640,2048]{1,0:T(8,128)(2,1)S(1)} %bitcast.28, s32[1024]{0:T(1024)S(1)} %pad_clamp_fusion), kind=kCustom, calls=%fused_computation | custom fusion | bytes 5245440 | tf_op jit(solution)/shard_map/jit(_take)/gather | solution.py:53
  43.2 0.0 copy-done.3
  43.2 0.1 fusion.53
  43.3 0.1 concatenate.12
  43.4 1.4 %collective-permute-done.4 = bf16[256,512]{1,0:T(8,128)(2,1)S(1)} collective-permute-done((bf16[256,512]{1,0:T(8,128)(2,1)S(1)}, bf16[256,512]{1,0:T(8,128)(2,1)S(1)}, u32[]{:S(2)}, u32[]{:S(2)}) %collective-permute-start.4) | collective-permute-done | bytes 262176 | tf_op jit(solution)/shard_map/ppermute | solution.py:28
  44.8 6.1 %collective-permute-done.5 = bf16[256,512]{1,0:T(8,128)(2,1)} collective-permute-done((bf16[256,512]{1,0:T(8,128)(2,1)S(1)}, bf16[256,512]{1,0:T(8,128)(2,1)}, u32[]{:S(2)}, u32[]{:S(2)}) %collective-permute-start.5) | collective-permute-done | bytes 262176 | tf_op jit(solution)/shard_map/ppermute | solution.py:28
  50.9 0.0 collective-permute-done.6
  50.9 1.1 %pad_maximum_fusion = bf16[256,2048]{1,0:T(8,128)(2,1)S(1)} fusion(bf16[256,512]{1,0:T(8,128)(2,1)S(1)} %collective-permute-done.6, bf16[256,512]{1,0:T(8,128)(2,1)} %collective-permute-done.5, bf16[256,512]{1,0:T(8,128)(2,1)S(1)} %collective-permute-done.4, bf16[256,512]{1,0:T(8,128)(2,1)S(1)} %fusion.5), kind=kLoop, calls=%fused_computation.14 | loop fusion | flops 4194304 | bytes 2097152 | tf_op jit(solution)/shard_map/concatenate | solution.py:59
  52.0 0.1 collective-permute-start.7
  52.1 1.5 %fusion.22 = f32[256,640]{1,0:T(8,128)S(1)} fusion(bf16[256,512]{1,0:T(8,128)(2,1)S(1)} %fusion.5, bf16[640,2048]{1,0:T(8,128)(2,1)} %gather_fusion, s32[]{:T(128)S(6)} %select_n.108), kind=kOutput, calls=%fused_computation.32 | convolution fusion | flops 167772160 | bytes 1572868 | tf_op jit(solution)/shard_map/qk,rk->qr/dot_general | solution.py:67
  53.6 0.0 copy-done.1
  53.6 0.4 fusion.18
  54.0 0.4 convolution_add_fusion.2
  54.4 0.3 collective-permute-done.7
  54.7 0.4 fusion.13
  55.1 0.4 fusion.11
  55.5 0.4 fusion.15
  55.9 0.4 fusion.4
  56.4 1.4 %fusion.3 = bf16[256,640]{1,0:T(8,128)(2,1)S(1)} fusion(f32[256,640]{1,0:T(8,128)S(1)} %fusion.11, f32[256,640]{1,0:T(8,128)S(1)} %fusion.15, f32[256,640]{1,0:T(8,128)S(1)} %fusion.18, bf16[256,512]{1,0:T(8,128)(2,1)} %collective-permute-done.5, bf16[640,2048]{1,0:T(8,128)(2,1)S(1)} %copy-done.1, s32[]{:T(128)S(6)} %select_n.108), kind=kOutput, calls=%fused_computation.8 | convolution fusion | flops 168427520 | bytes 3211268 | tf_op jit(solution)/shard_map/qk,rk->qr/dot_general | solution.py:67
  57.8 0.3 convolution_convert_fusion.2
  58.1 2.2 %collective-permute-start.8 = (bf16[128,640]{1,0:T(8,128)(2,1)S(1)}, bf16[128,640]{1,0:T(8,128)(2,1)S(1)}, u32[]{:S(2)}, u32[]{:S(2)}) collective-permute-start(bf16[128,640]{1,0:T(8,128)(2,1)S(1)} %convolution_convert_fusion.2), channel_id=1, source_target_pairs={{0,4},{4,0},{8,12},{12,8},{1,5},{5,1},{9,13},{13,9},{2,6},{6,2},{1... | collective-permute-start | bytes 491528 | tf_op jit(solution)/shard_map/ppermute | solution.py:28
  60.3 0.3 convolution_convert_fusion.1
  60.6 1.1 %collective-permute-start.9 = (bf16[128,640]{1,0:T(8,128)(2,1)S(1)}, bf16[128,640]{1,0:T(8,128)(2,1)S(1)}, u32[]{:S(2)}, u32[]{:S(2)}) collective-permute-start(bf16[128,640]{1,0:T(8,128)(2,1)S(1)} %convolution_convert_fusion.1), channel_id=1, source_target_pairs={{0,8},{4,12},{8,0},{12,4},{1,9},{5,13},{9,1},{13,5},{2,10},{6,14},... | collective-permute-start | bytes 491528 | tf_op jit(solution)/shard_map/ppermute | solution.py:28
  61.7 0.3 convolution_convert_fusion
  62.0 1.5 %collective-permute-start.10 = (bf16[128,640]{1,0:T(8,128)(2,1)S(1)}, bf16[128,640]{1,0:T(8,128)(2,1)S(1)}, u32[]{:S(2)}, u32[]{:S(2)}) collective-permute-start(bf16[128,640]{1,0:T(8,128)(2,1)S(1)} %convolution_convert_fusion), channel_id=1, source_target_pairs={{0,12},{4,8},{8,4},{12,0},{1,13},{5,9},{9,5},{13,1},{2,14},{6,10},... | collective-permute-start | bytes 491528 | tf_op jit(solution)/shard_map/ppermute | solution.py:28
  63.5 4.0 %collective-permute-done.8 = bf16[128,640]{1,0:T(8,128)(2,1)S(1)} collective-permute-done((bf16[128,640]{1,0:T(8,128)(2,1)S(1)}, bf16[128,640]{1,0:T(8,128)(2,1)S(1)}, u32[]{:S(2)}, u32[]{:S(2)}) %collective-permute-start.8) | collective-permute-done | bytes 163872 | tf_op jit(solution)/shard_map/ppermute | solution.py:28
  67.6 8.1 %collective-permute-done.9 = bf16[128,640]{1,0:T(8,128)(2,1)S(1)} collective-permute-done((bf16[128,640]{1,0:T(8,128)(2,1)S(1)}, bf16[128,640]{1,0:T(8,128)(2,1)S(1)}, u32[]{:S(2)}, u32[]{:S(2)}) %collective-permute-start.9) | collective-permute-done | bytes 163872 | tf_op jit(solution)/shard_map/ppermute | solution.py:28
  75.7 0.0 collective-permute-done.10
  75.7 1.0 %convert_add_fusion = f32[128,640]{1,0:T(8,128)} fusion(bf16[128,640]{1,0:T(8,128)(2,1)S(1)} %collective-permute-done.10, bf16[128,640]{1,0:T(8,128)(2,1)S(1)} %collective-permute-done.9, bf16[128,640]{1,0:T(8,128)(2,1)S(1)} %collective-permute-done.8, s32[512]{0:T(512)S(1)} %concatenate.12, s32[128]{0:T(128)S(1)} %iota_add_fusion.3, ...), kind=kOutput, calls=%fused_computation.35 | convolution fusion | flops 85753856 | bytes 1477120 | tf_op jit(solution)/shard_map/oq,qr->or/dot_general | solution.py:84
  (14 shorter events, 0.2 us)
Async XLA Ops:
  0.0 39.1 %copy-start = (bf16[640,1,2048]{2,0,1:T(8,128)(2,1)S(1)}, bf16[640,1,2048]{2,0,1:T(8,128)(2,1)}, u32[]{:S(2)}) copy-start(bf16[640,1,2048]{2,0,1:T(8,128)(2,1)} %param.8) | copy-start | bytes 7864324
  12.5 8.1 %collective-permute-start = (bf16[64,1024]{1,0:T(8,128)(2,1)S(1)}, bf16[64,1024]{1,0:T(8,128)(2,1)S(1)}, u32[]{:S(2)}, u32[]{:S(2)}) collective-permute-start(bf16[64,1024]{1,0:T(8,128)(2,1)S(1)} %bitcast.31), channel_id=1, source_target_pairs={{0,4},{4,0},{8,12},{12,8},{1,5},{5,1},{9,13},{13,9},{2,6},{6,2},{1... | collective-permute-start | bytes 393224 | tf_op jit(solution)/shard_map/ppermute | solution.py:28
  15.6 12.9 %collective-permute-start.1 = (bf16[64,1024]{1,0:T(8,128)(2,1)S(1)}, bf16[64,1024]{1,0:T(8,128)(2,1)S(1)}, u32[]{:S(2)}, u32[]{:S(2)}) collective-permute-start(bf16[64,1024]{1,0:T(8,128)(2,1)S(1)} %bitcast.32), channel_id=1, source_target_pairs={{0,8},{4,12},{8,0},{12,4},{1,9},{5,13},{9,1},{13,5},{2,10},{6,14},... | collective-permute-start | bytes 393224 | tf_op jit(solution)/shard_map/ppermute | solution.py:28
  18.3 10.2 %collective-permute-start.2 = (bf16[64,1024]{1,0:T(8,128)(2,1)S(1)}, bf16[64,1024]{1,0:T(8,128)(2,1)}, u32[]{:S(2)}, u32[]{:S(2)}) collective-permute-start(bf16[64,1024]{1,0:T(8,128)(2,1)S(1)} %bitcast.33), channel_id=1, source_target_pairs={{0,12},{4,8},{8,4},{12,0},{1,13},{5,9},{9,5},{13,1},{2,14},{6,10},... | collective-permute-start | bytes 393224 | tf_op jit(solution)/shard_map/ppermute | solution.py:28
  30.3 2.1 %collective-permute-start.3 = (bf16[256,1024]{1,0:T(8,128)(2,1)}, bf16[256,1024]{1,0:T(8,128)(2,1)S(1)}, u32[]{:S(2)}, u32[]{:S(2)}) collective-permute-start(bf16[256,1024]{1,0:T(8,128)(2,1)} %pad_maximum_fusion.2), channel_id=1, source_target_pairs={{0,1},{1,0},{2,3},{3,2},{4,5},{5,4},{6,7},{7,6},{8,9},{9,8},{10,11... | collective-permute-start | bytes 1572872 | tf_op jit(solution)/shard_map/ppermute | solution.py:28
  30.3 3.8 %copy-start.2 = (bf16[1,512,2048]{2,1,0:T(8,128)(2,1)S(1)}, bf16[1,512,2048]{2,1,0:T(8,128)(2,1)}, u32[]{:S(2)}) copy-start(bf16[1,512,2048]{2,1,0:T(8,128)(2,1)} %param.7) | copy-start | bytes 6291460
  34.1 5.0 %copy-start.4 = (s32[640]{0:T(1024)S(1)}, s32[640]{0:T(1024)}, u32[]{:S(2)}) copy-start(s32[640]{0:T(1024)} %param.11) | copy-start | bytes 7684
  35.5 9.2 %collective-permute-start.4 = (bf16[256,512]{1,0:T(8,128)(2,1)S(1)}, bf16[256,512]{1,0:T(8,128)(2,1)S(1)}, u32[]{:S(2)}, u32[]{:S(2)}) collective-permute-start(bf16[256,512]{1,0:T(8,128)(2,1)S(1)} %fusion.5), channel_id=1, source_target_pairs={{0,2},{2,0},{16,18},{18,16},{1,3},{3,1},{17,19},{19,17},{4,6},{6,4... | collective-permute-start | bytes 786440 | tf_op jit(solution)/shard_map/ppermute | solution.py:28
  37.1 13.8 %collective-permute-start.5 = (bf16[256,512]{1,0:T(8,128)(2,1)S(1)}, bf16[256,512]{1,0:T(8,128)(2,1)}, u32[]{:S(2)}, u32[]{:S(2)}) collective-permute-start(bf16[256,512]{1,0:T(8,128)(2,1)S(1)} %fusion.5), channel_id=1, source_target_pairs={{0,16},{2,18},{16,0},{18,2},{1,17},{3,19},{17,1},{19,3},{4,20},{6,... | collective-permute-start | bytes 786440 | tf_op jit(solution)/shard_map/ppermute | solution.py:28
  38.3 12.6 %collective-permute-start.6 = (bf16[256,512]{1,0:T(8,128)(2,1)S(1)}, bf16[256,512]{1,0:T(8,128)(2,1)S(1)}, u32[]{:S(2)}, u32[]{:S(2)}) collective-permute-start(bf16[256,512]{1,0:T(8,128)(2,1)S(1)} %fusion.5), channel_id=1, source_target_pairs={{0,18},{2,16},{16,2},{18,0},{1,19},{3,17},{17,3},{19,1},{4,22},{6,... | collective-permute-start | bytes 786440 | tf_op jit(solution)/shard_map/ppermute | solution.py:28
  39.1 4.1 %copy-start.3 = (s32[512]{0:T(512)S(1)}, s32[512]{0:T(512)}, u32[]{:S(2)}) copy-start(s32[512]{0:T(512)} %param.9) | copy-start | bytes 6148
  43.4 10.2 %copy-start.1 = (bf16[640,2048]{1,0:T(8,128)(2,1)S(1)}, bf16[640,2048]{1,0:T(8,128)(2,1)}, u32[]{:S(2)}) copy-start(bf16[640,2048]{1,0:T(8,128)(2,1)} %gather_fusion) | copy-start | bytes 7864324
  52.0 2.7 %collective-permute-start.7 = (bf16[256,2048]{1,0:T(8,128)(2,1)S(1)}, bf16[256,2048]{1,0:T(8,128)(2,1)S(1)}, u32[]{:S(2)}, u32[]{:S(2)}) collective-permute-start(bf16[256,2048]{1,0:T(8,128)(2,1)S(1)} %pad_maximum_fusion), channel_id=1, source_target_pairs={{0,1},{1,0},{2,3},{3,2},{4,5},{5,4},{6,7},{7,6},{8,9},{9,8},{10,11... | collective-permute-start | bytes 3145736 | tf_op jit(solution)/shard_map/ppermute | solution.py:28
  58.1 9.4 %collective-permute-start.8 = (bf16[128,640]{1,0:T(8,128)(2,1)S(1)}, bf16[128,640]{1,0:T(8,128)(2,1)S(1)}, u32[]{:S(2)}, u32[]{:S(2)}) collective-permute-start(bf16[128,640]{1,0:T(8,128)(2,1)S(1)} %convolution_convert_fusion.2), channel_id=1, source_target_pairs={{0,4},{4,0},{8,12},{12,8},{1,5},{5,1},{9,13},{13,9},{2,6},{6,2},{1... | collective-permute-start | bytes 491528 | tf_op jit(solution)/shard_map/ppermute | solution.py:28
  60.6 15.1 %collective-permute-start.9 = (bf16[128,640]{1,0:T(8,128)(2,1)S(1)}, bf16[128,640]{1,0:T(8,128)(2,1)S(1)}, u32[]{:S(2)}, u32[]{:S(2)}) collective-permute-start(bf16[128,640]{1,0:T(8,128)(2,1)S(1)} %convolution_convert_fusion.1), channel_id=1, source_target_pairs={{0,8},{4,12},{8,0},{12,4},{1,9},{5,13},{9,1},{13,5},{2,10},{6,14},... | collective-permute-start | bytes 491528 | tf_op jit(solution)/shard_map/ppermute | solution.py:28
  62.0 13.7 %collective-permute-start.10 = (bf16[128,640]{1,0:T(8,128)(2,1)S(1)}, bf16[128,640]{1,0:T(8,128)(2,1)S(1)}, u32[]{:S(2)}, u32[]{:S(2)}) collective-permute-start(bf16[128,640]{1,0:T(8,128)(2,1)S(1)} %convolution_convert_fusion), channel_id=1, source_target_pairs={{0,12},{4,8},{8,4},{12,0},{1,13},{5,9},{9,5},{13,1},{2,14},{6,10},... | collective-permute-start | bytes 491528 | tf_op jit(solution)/shard_map/ppermute | solution.py:28
